TPU v7x, 32 devices: a whole 2x2x4 slice. The times are simulated.
32 devices in a mesh: ctx: 2 (over y), branch: 4 (over z), head: 4 (over x, core).
Axes of the slice: x: 2, y: 2, z: 4, core: 2. Of those that a mesh axis runs over, the one named last changes fastest.
Arguments:
- queries: bfloat16 [8, 128, 4096], P(('ctx', 'branch'), None, 'head'), may hold values from -320 to 320
- branch_keys: bfloat16 [8, 128, 512], P(('ctx', 'branch'), None, 'head'), may hold values from -12 to 12
- branch_value_rows: bfloat16 [8, 128, 512], P(('ctx', 'branch'), None, 'head'), may hold values from -6 to 6
- trunk_key_rows: bfloat16 [192, 512], P('ctx', 'head'), may hold values from -6 to 6
- trunk_value_rows: bfloat16 [192, 512], P('ctx', 'head'), may hold values from -6 to 6
- attn_out: bfloat16 [8, 128, 4096], P(('ctx', 'branch'), None, 'head'), may hold values from -2 to 2
- out_grad: bfloat16 [8, 128, 4096], P(('ctx', 'branch'), None, 'head'), may hold values from -6 to 6
- block_mask: int32 [8, 1, 3], P(('ctx', 'branch')), may hold values from 0 to 1, as said below
Outputs:
- query_grad: bfloat16 [8, 128, 4096], P(('ctx', 'branch'), None, 'head')
- branch_kv_grad: bfloat16 [8, 128, 1024], P(('ctx', 'branch'), None, 'head')
- trunk_kv_grad: bfloat16 [192, 1024], P(('ctx', 'branch'), 'head')
Inputs may be any that keep to these rules, and one draw needn't show every extreme that they name: `block_mask`: each entry is 0 or 1; columns 0 to 1 are the trunk's blocks, the rest the branch's own blocks, of which those on or above the query block's diagonal are not read. Every query block of every branch sees at least one trunk block. The share of ones differs from branch to branch.
All inputs are finite; a program needn't handle non-finite values.
Results may differ from a plain program's by a relative error of at most 0.017.
Values may be sent and summed in bfloat16 or wider, within the bound.
No kernel may reach another device: no remote copies, remote signals or barrier semaphores. Data moves between devices by JAX's collectives and lax.ppermute only.
A program may use at most 64 MiB of HBM per device.

v0:
```python
import math

import jax
import jax.numpy as jnp
from jax import lax
from jax.sharding import PartitionSpec as P

HEAD_WIDTH = 128
BLK = 128


masked_fill = -1e30


def head_scores(query_row_block, key_row_block, score_scale):
    return (
        jnp.einsum(
            "igd,kd->gik", query_row_block, key_row_block, preferred_element_type=jnp.float32
        )
        * score_scale
    )


def block_gradients(
    query_row_block,
    gradient_rows,
    key_row_block,
    value_rows,
    allowed,
    log_total,
    out_dot,
    score_scale,
):
    scores = head_scores(query_row_block, key_row_block, score_scale)
    weights = jnp.exp(jnp.where(allowed[None], scores, masked_fill) - log_total)
    weights_low = weights.astype(jnp.bfloat16)
    grad_weights = jnp.einsum(
        "igd,kd->gik", gradient_rows, value_rows, preferred_element_type=jnp.float32
    )
    grad_scores = (weights * (grad_weights - out_dot)).astype(jnp.bfloat16)
    query_portion = jnp.einsum(
        "gik,kd->igd", grad_scores, key_row_block, preferred_element_type=jnp.float32
    )
    key_gradient = (
        jnp.einsum("gik,igd->kd", grad_scores, query_row_block, preferred_element_type=jnp.float32)
        * score_scale
    )
    value_gradient = jnp.einsum(
        "gik,igd->kd", weights_low, gradient_rows, preferred_element_type=jnp.float32
    )
    return (query_portion, jnp.concatenate([key_gradient, value_gradient], axis=1))


def trunk_allowed(trunk_mask, offset, key_count, branch_len):
    tokens = offset + jnp.arange(key_count, dtype=jnp.int32)
    blocks = jnp.arange(trunk_mask.shape[1], dtype=jnp.int32)
    onehot = (tokens[None, :] // BLK == blocks[:, None]).astype(jnp.float32)
    visible = jnp.dot(trunk_mask, onehot, preferred_element_type=jnp.float32) > 0.5
    spread = jnp.broadcast_to(visible[:, None, :], (visible.shape[0], BLK, key_count))
    return spread.reshape(branch_len, key_count)


def branch_allowed(branch_mask, branch_len):
    block_count = branch_mask.shape[0]
    spread = jnp.broadcast_to(
        branch_mask[:, None, :, None] > 0, (block_count, BLK, block_count, BLK)
    ).reshape(branch_len, branch_len)
    position = jnp.arange(branch_len, dtype=jnp.int32)
    query_block = position[:, None] // BLK
    key_block = position[None, :] // BLK
    earlier = (key_block < query_block) & spread
    causal = (key_block == query_block) & (position[None, :] <= position[:, None])
    return earlier | causal


def shards(
    queries,
    branch_keys,
    branch_value_rows,
    trunk_key_rows,
    trunk_value_rows,
    attn_out,
    out_grad,
    block_mask,
):
    branch_len = queries.shape[1]
    group_width = queries.shape[2] // HEAD_WIDTH
    score_scale = 1.0 / math.sqrt(HEAD_WIDTH)
    query_row_block = queries[0].reshape(branch_len, group_width, HEAD_WIDTH)
    gradient_rows = out_grad[0].reshape(branch_len, group_width, HEAD_WIDTH)
    output_rows = attn_out[0].reshape(branch_len, group_width, HEAD_WIDTH)
    branch_own_keys = branch_keys[0]
    branch_own_values = branch_value_rows[0]
    mask_rows = block_mask[0]
    query_blocks = branch_len // BLK
    trunk_blocks = mask_rows.shape[1] - query_blocks
    trunk_mask = mask_rows[:, :trunk_blocks].astype(jnp.float32)
    own_allowed = branch_allowed(mask_rows[:, trunk_blocks:], branch_len)
    own_scores = jnp.where(
        own_allowed[None], head_scores(query_row_block, branch_own_keys, score_scale), masked_fill
    )
    row_max = jnp.max(own_scores, axis=2, keepdims=True)
    row_total = jnp.sum(jnp.exp(own_scores - row_max), axis=2, keepdims=True)
    trunk_rows, trunk_vals = (
        lax.all_gather(trunk_key_rows, "ctx", axis=0, tiled=True),
        lax.all_gather(trunk_value_rows, "ctx", axis=0, tiled=True),
    )
    trunk_len = trunk_rows.shape[0]
    block_len = math.gcd(512, trunk_len)
    block_total = trunk_len // block_len
    key_blocks = trunk_rows.reshape(block_total, block_len, HEAD_WIDTH)
    value_blocks = trunk_vals.reshape(block_total, block_len, HEAD_WIDTH)
    offsets = jnp.arange(block_total, dtype=jnp.int32) * block_len

    def stats_step(running, inputs):
        run_max, run_total = running
        key_block, offset = inputs
        allowed = trunk_allowed(trunk_mask, offset, block_len, branch_len)
        scores = jnp.where(
            allowed[None], head_scores(query_row_block, key_block, score_scale), masked_fill
        )
        new_max = jnp.maximum(run_max, jnp.max(scores, axis=2, keepdims=True))
        new_total = run_total * jnp.exp(run_max - new_max) + jnp.sum(
            jnp.exp(scores - new_max), axis=2, keepdims=True
        )
        return ((new_max, new_total), None)

    (row_max, row_total), ignored = lax.scan(
        stats_step, (row_max, row_total), (key_blocks, offsets)
    )
    log_total = row_max + jnp.log(row_total)
    out_dot = jnp.sum(
        gradient_rows.astype(jnp.float32) * output_rows.astype(jnp.float32), axis=2
    ).T[:, :, None]
    own_query, own_grad = block_gradients(
        query_row_block,
        gradient_rows,
        branch_own_keys,
        branch_own_values,
        own_allowed,
        log_total,
        out_dot,
        score_scale,
    )

    def grad_step(query_sum, inputs):
        key_block, value_block, offset = inputs
        allowed = trunk_allowed(trunk_mask, offset, block_len, branch_len)
        query_portion, key_value_pair = block_gradients(
            query_row_block,
            gradient_rows,
            key_block,
            value_block,
            allowed,
            log_total,
            out_dot,
            score_scale,
        )
        return (query_sum + query_portion, key_value_pair)

    query_sum, trunk_grad = lax.scan(grad_step, own_query, (key_blocks, value_blocks, offsets))
    query_out = (
        (query_sum * score_scale)
        .astype(jnp.bfloat16)
        .reshape(1, branch_len, group_width * HEAD_WIDTH)
    )
    branch_out = own_grad.astype(jnp.bfloat16)[None]
    trunk_term = lax.optimization_barrier(
        trunk_grad.reshape(trunk_len, 2 * HEAD_WIDTH).astype(jnp.bfloat16)
    ).astype(jnp.float32)
    reduced = lax.psum_scatter(
        trunk_term.astype(jnp.bfloat16), "ctx", scatter_dimension=0, tiled=True
    )
    trunk_out = lax.psum_scatter(reduced, "branch", scatter_dimension=0, tiled=True).astype(
        jnp.float32
    )
    return (query_out, branch_out, trunk_out.astype(jnp.bfloat16))


def solution(mesh):
    return jax.shard_map(
        shards,
        mesh=mesh,
        in_specs=(
            P(("ctx", "branch"), None, "head"),
            P(("ctx", "branch"), None, "head"),
            P(("ctx", "branch"), None, "head"),
            P("ctx", "head"),
            P("ctx", "head"),
            P(("ctx", "branch"), None, "head"),
            P(("ctx", "branch"), None, "head"),
            P(("ctx", "branch"), None, None),
        ),
        out_specs=(
            P(("ctx", "branch"), None, "head"),
            P(("ctx", "branch"), None, "head"),
            P(("ctx", "branch"), "head"),
        ),
        check_vma=False,
    )
```

profile of v0, /device:TPU:0, one launch (start us, length us, event | category | flops | bytes accessed | tf_op | source)
XLA Modules:
  0.0 79.4 jit_solution(5890720401216771830)
XLA Ops:
  7.2 0.6 copy-done.5
  7.8 0.6 slice.6
  8.5 5.7 %all_gather.6 = bf16[192,128]{1,0:T(8,128)(2,1)S(1)} all-gather(bf16[96,128]{1,0:T(8,128)(2,1)} %param.15), channel_id=1, replica_groups=mesh['ctx'=2,'branch'=4,'head'=4] {'ctx'}, dimensions={0}, use_global_device_ids=true | all-gather | bytes 73728 | tf_op jit(solution)/shard_map/all_gather | solution.py:105
  14.2 4.5 %all_gather.7 = bf16[192,128]{1,0:T(8,128)(2,1)S(1)} all-gather(bf16[96,128]{1,0:T(8,128)(2,1)S(1)} %copy-done.4), channel_id=1, replica_groups=mesh['ctx'=2,'branch'=4,'head'=4] {'ctx'}, dimensions={0}, use_global_device_ids=true | all-gather | bytes 73728 | tf_op jit(solution)/shard_map/all_gather | solution.py:106
  18.7 1.1 %copy.19 = bf16[1,128,1024]{1,2,0:T(8,128)(2,1)S(1)} copy(bf16[1,128,1024]{2,1,0:T(8,128)(2,1)} %param.12) | data formatting | bytes 524288 | tf_op args[0]
  20.0 0.8 copy-done.1
  20.9 0.8 copy-done.2
  21.9 0.2 copy.28
  22.9 0.2 fusion.55
  23.3 5.1 %while.28 = (s32[]{:T(128)}, f32[8,128,1]{1,0,2:T(8,128)S(1)}, f32[8,128,1]{1,0,2:T(8,128)S(1)}, s32[3]{0:T(128)S(1)}, bf16[1,2]{1,0:T(2,128)(2,1)S(1)}, /*index...) while((s32[]{:T(128)}, f32[8,128,1]{1,0,2:T(8,128)S(1)}, ...), condition=%wide.region_5.6_spmd, body=%wide.region_2.5_spmd.sunk | while | flops 17108416 | bytes 857269 | solution.py:128
  23.3 0.6 dynamic_slice.57
  23.9 0.7 and_select_fusion.5
  24.6 0.2 fusion.96
  25.0 0.6 dynamic_slice.57
  25.6 0.7 and_select_fusion.5
  26.3 0.2 fusion.96
  26.7 0.6 dynamic_slice.57
  27.3 0.7 and_select_fusion.5
  28.1 0.2 fusion.96
  28.4 0.2 fusion.39
  28.6 0.3 convolution_bitcast_fusion.6
  28.9 0.2 copy.26
  29.1 9.3 %while.29 = (s32[]{:T(128)}, f32[128,8,128]{0,2,1:T(8,128)S(1)}, bf16[3,64,256]{2,1,0:T(8,128)(2,1)}, bf16[3,64,128]{2,1,0:T(8,128)(2,1)S(1)}, s32[3]{0:T(128)S(...) while((s32[]{:T(128)}, f32[128,8,128]{0,2,1:T(8,128)S(1)}, ...), condition=%wide.region_8.9_spmd, body=%wide.region_7.8_spmd.sunk | while | flops 84559296 | bytes 3433697 | solution.py:161
  29.1 0.6 dynamic_slice.61
  29.7 0.7 and_select_fusion.6
  30.5 0.2 fusion.110
  30.9 0.2 fusion.111
  31.3 0.6 fusion.114
  31.9 0.3 fusion.112
  32.2 0.6 dynamic_slice.61
  32.8 0.7 and_select_fusion.6
  33.6 0.2 fusion.110
  33.8 0.2 convolution_bitcast_fusion.11
  34.0 0.2 fusion.111
  34.4 0.6 fusion.114
  35.0 0.3 fusion.112
  35.3 0.6 dynamic_slice.61
  35.9 0.7 and_select_fusion.6
  36.7 0.2 fusion.110
  37.1 0.2 fusion.111
  37.5 0.6 fusion.114
  38.1 0.3 fusion.112
  38.5 0.2 fusion.44
  38.7 0.2 fusion.43
  39.1 11.4 %reduce-scatter.3.cloned.1.call-done = bf16[96,256]{1,0:T(8,128)(2,1)} async-done(((bf16[192,256]{1,0:T(8,128)(2,1)}), bf16[96,256]{1,0:T(8,128)(2,1)}) %reduce-scatter.3.cloned.1.call-update) | async-done | bytes 49168 | tf_op jit(solution)/shard_map/reduce_scatter | solution.py:171
  50.5 0.7 copy.32
  51.2 0.8 %copy.38 = bf16[1,128,1024]{2,1,0:T(8,128)(2,1)} copy(bf16[1,128,1024]{1,2,0:T(8,128)(2,1)S(1)} %bitcast.209) | data formatting | bytes 524288 | tf_op jit(solution)/shard_map/reshape | solution.py:165
  52.1 20.5 %reduce-scatter.5.cloned.1.call-done = bf16[24,256]{1,0:T(8,128)(2,1)} async-done(((bf16[96,256]{1,0:T(8,128)(2,1)}), bf16[24,256]{1,0:T(8,128)(2,1)}) %reduce-scatter.5.cloned.1.call-update) | async-done | bytes 12304 | tf_op jit(solution)/shard_map/reduce_scatter | solution.py:174
  (49 shorter events, 2.9 us)
Async XLA Ops:
  7.2 15.7 %copy-start = (bf16[1,128,128]{2,1,0:T(8,128)(2,1)S(1)}, bf16[1,128,128]{2,1,0:T(8,128)(2,1)}, u32[]{:S(2)}) copy-start(bf16[1,128,128]{2,1,0:T(8,128)(2,1)} %param.13) | copy-start | bytes 98308
  7.2 0.7 copy-start.5
  7.2 43.2 %reduce-scatter.3.cloned.1.call-start = ((), (), s32[]{:S(2)}) async-start(), calls=%async_computation.2 | async-start | bytes 147456 | tf_op jit(solution)/shard_map/reduce_scatter | solution.py:171
  8.4 5.7 %copy-start.4 = (bf16[96,128]{1,0:T(8,128)(2,1)S(1)}, bf16[96,128]{1,0:T(8,128)(2,1)}, u32[]{:S(2)}) copy-start(bf16[96,128]{1,0:T(8,128)(2,1)} %param.16) | copy-start | bytes 73732
  19.8 1.0 %copy-start.1 = (bf16[1,128,1024]{2,1,0:T(8,128)(2,1)S(1)}, bf16[1,128,1024]{2,1,0:T(8,128)(2,1)}, u32[]{:S(2)}) copy-start(bf16[1,128,1024]{2,1,0:T(8,128)(2,1)} %param.17) | copy-start | bytes 786436
  20.8 0.9 %copy-start.2 = (bf16[1,128,1024]{2,1,0:T(8,128)(2,1)S(1)}, bf16[1,128,1024]{2,1,0:T(8,128)(2,1)}, u32[]{:S(2)}) copy-start(bf16[1,128,1024]{2,1,0:T(8,128)(2,1)} %param.18) | copy-start | bytes 786436
  23.2 5.2 %copy-start.3 = (bf16[1,128,128]{2,1,0:T(8,128)(2,1)S(1)}, bf16[1,128,128]{2,1,0:T(8,128)(2,1)}, u32[]{:S(2)}) copy-start(bf16[1,128,128]{2,1,0:T(8,128)(2,1)} %param.14) | copy-start | bytes 98308
  38.4 34.1 %reduce-scatter.5.cloned.1.call-start = ((), (), s32[]{:S(2)}) async-start(), calls=%async_computation.3 | async-start | bytes 61440 | tf_op jit(solution)/shard_map/reduce_scatter | solution.py:174
Sparse Core Ops, SparseCore 0:
  38.6 11.8 reduce-scatter.2
  53.2 19.2 reduce-scatter.4
where the time goes:
time: 79.8 us; the launch traced here: 79.4 us
  waiting for transfers between devices  31.9 us (40%)
  between operations  14.9 us (19%)
  blocking collectives  10.2 us (13%)
  local copies, waits for them, and re-layouts  9.88 us (12%)
  other arithmetic  6.35 us (8%)
  matrix products  5.74 us (7%)
    reduce_scatter x1, waiting for transfers between devices, shards(): lax.psum_scatter(reduced, 'branch', scatter_dimension=0, tiled=True)  20.5 us
    reduce_scatter x1, waiting for transfers between devices, shards(): lax.psum_scatter(trunk_term.astype(jnp.bfloat16), 'ctx', scatter_dimensio...  11.4 us
    all_gather x1, blocking collectives, shards(): lax.all_gather(trunk_key_rows, 'ctx', axis=0, tiled=True)  5.73 us
    all_gather x1, blocking collectives, shards(): lax.all_gather(trunk_value_rows, 'ctx', axis=0, tiled=True)  4.48 us
    unnamed x16, local copies, waits for them, and re-layouts  4.36 us
    select_n x6, other arithmetic, trunk_allowed(): onehot = (tokens[None, :] // BLK == blocks[:, None]).astype(jnp.float32)  3.92 us
    dynamic_slice x6, local copies, waits for them, and re-layouts, shards(): lax.scan(stats_step, (row_max, row_total), (key_blocks, offsets))  3.52 us
    dynamic_update_slice x3, other arithmetic, shards(): lax.scan(grad_step, own_query, (key_blocks, value_blocks, offsets))  1.88 us
  transfers between devices with their start and end apart: 2, of which 2 were waited for; matrix products, arithmetic and copies ran while one was open for 3% of the time, Pallas kernels for 0%

commit v1 on v0

--- a/solution.py
+++ b/solution.py
@@ -1,8 +1,11 @@
+import functools
 import math
 
 import jax
 import jax.numpy as jnp
 from jax import lax
+from jax.experimental import pallas as pl
+from jax.experimental.pallas import tpu as pltpu
 from jax.sharding import PartitionSpec as P
 
 HEAD_WIDTH = 128
@@ -10,6 +13,271 @@
 
 
 masked_fill = -1e30
+VMEM = pl.BlockSpec(memory_space=pltpu.VMEM)
+SMEM = pl.BlockSpec(memory_space=pltpu.SMEM)
+NT = (((1,), (1,)), ((), ()))
+TN = (((0,), (0,)), ((), ()))
+
+
+def mm(a, b, dims=(((1,), (0,)), ((), ()))):
+    return lax.dot_general(a, b, dims, preferred_element_type=jnp.float32)
+
+
+def stacked(ref, chunk, heads):
+    return jnp.concatenate(
+        [
+            ref[0, :, j * HEAD_WIDTH : (j + 1) * HEAD_WIDTH]
+            for j in range(chunk * heads, (chunk + 1) * heads)
+        ],
+        axis=0,
+    )
+
+
+def trunk_visible(mask_ref, part_ref, shape, trunk_blocks):
+    token = part_ref[0] * shape[0] + lax.broadcasted_iota(jnp.int32, shape, 0)
+    visible = jnp.zeros(shape, jnp.int32)
+    for block in range(trunk_blocks):
+        inside = (token >= block * BLK) & (token < (block + 1) * BLK)
+        visible = jnp.where(inside, mask_ref[0, 0, block], visible)
+    return visible > 0
+
+
+def own_kernel(
+    trunk_blocks,
+    heads,
+    mask_ref,
+    part_ref,
+    q_ref,
+    g_ref,
+    o_ref,
+    bk_ref,
+    bv_ref,
+    tk_ref,
+    tv_ref,
+    e_ref,
+    gs_ref,
+    stat_ref,
+):
+    rows = q_ref.shape[1]
+    own = bk_ref.shape[1]
+    scale = 1.0 / math.sqrt(HEAD_WIDTH)
+    keys = jnp.concatenate([bk_ref[0], tk_ref[...]], axis=0)
+    values = jnp.concatenate([bv_ref[0], tv_ref[...]], axis=0)
+    width = heads * rows
+    key_row = lax.broadcasted_iota(jnp.int32, (own, rows), 0)
+    query_row = lax.broadcasted_iota(jnp.int32, (own, rows), 1)
+    causal = key_row <= query_row
+    visible = trunk_visible(mask_ref, part_ref, (tk_ref.shape[0], rows), trunk_blocks)
+    allowed = jnp.concatenate([jnp.concatenate([causal, visible], axis=0)] * heads, axis=1)
+    ones = jnp.ones((8, HEAD_WIDTH), jnp.bfloat16)
+    for chunk in range(q_ref.shape[2] // (heads * HEAD_WIDTH)):
+        at = slice(chunk * width, (chunk + 1) * width)
+        q = stacked(q_ref, chunk, heads)
+        g = stacked(g_ref, chunk, heads)
+        prod = g.astype(jnp.float32) * stacked(o_ref, chunk, heads).astype(jnp.float32)
+        high = prod.astype(jnp.bfloat16)
+        low = (prod - high.astype(jnp.float32)).astype(jnp.bfloat16)
+        dot = mm(ones, high, NT) + mm(ones, low, NT)
+        s = jnp.where(allowed, mm(keys, q, NT) * scale, masked_fill)
+        top = jnp.max(s, axis=0, keepdims=True)
+        e = jnp.exp(s - top)
+        e_ref[:, at] = e
+        gs_ref[:, at] = e * (mm(values, g, NT) - dot[:1])
+        stat_ref[0:8, at] = jnp.broadcast_to(top, (8, width))
+        stat_ref[8:16, at] = jnp.broadcast_to(jnp.sum(e, axis=0, keepdims=True), (8, width))
+        stat_ref[16:24, at] = dot
+
+
+def far_kernel(
+    trunk_blocks,
+    heads,
+    mask_ref,
+    part_ref,
+    q_ref,
+    g_ref,
+    kv_ref,
+    stat_ref,
+    pair_ref,
+    ds_ref,
+    factor_ref,
+):
+    rows = q_ref.shape[1]
+    count = kv_ref.shape[0] // 2
+    scale = 1.0 / math.sqrt(HEAD_WIDTH)
+    keys = kv_ref[:count]
+    values = kv_ref[count:]
+    width = heads * rows
+    visible = trunk_visible(mask_ref, part_ref, (count, rows), trunk_blocks)
+    visible = jnp.concatenate([visible] * heads, axis=1)
+    dk = jnp.zeros((count, HEAD_WIDTH), jnp.float32)
+    dv = jnp.zeros((count, HEAD_WIDTH), jnp.float32)
+    for chunk in range(q_ref.shape[2] // (heads * HEAD_WIDTH)):
+        at = slice(chunk * width, (chunk + 1) * width)
+        q = stacked(q_ref, chunk, heads)
+        g = stacked(g_ref, chunk, heads)
+        s = jnp.where(visible, mm(keys, q, NT) * scale, masked_fill)
+        old = stat_ref[0:1, at]
+        top = jnp.maximum(old, jnp.max(s, axis=0, keepdims=True))
+        e = jnp.exp(s - top)
+        shrink = jnp.exp(old - top)
+        total = stat_ref[8:9, at] * shrink + jnp.sum(e, axis=0, keepdims=True)
+        inverse = 1.0 / total
+        w = e * inverse
+        ds = (w * (mm(values, g, NT) - stat_ref[16:17, at])).astype(jnp.bfloat16)
+        dk += mm(ds, q)
+        dv += mm(w.astype(jnp.bfloat16), g)
+        ds_ref[:, at] = ds
+        factor_ref[:, at] = jnp.broadcast_to(shrink * inverse, (8, width))
+    pair_ref[:, :HEAD_WIDTH] = (dk * scale).astype(jnp.bfloat16)
+    pair_ref[:, HEAD_WIDTH:] = dv.astype(jnp.bfloat16)
+
+
+def rest_kernel(
+    heads,
+    q_ref,
+    g_ref,
+    bk_ref,
+    tk_ref,
+    kv_ref,
+    e_ref,
+    gs_ref,
+    ds_ref,
+    factor_ref,
+    dq_ref,
+    branch_ref,
+    trunk_ref,
+):
+    rows = q_ref.shape[1]
+    own = bk_ref.shape[1]
+    count = tk_ref.shape[0]
+    scale = 1.0 / math.sqrt(HEAD_WIDTH)
+    keys = jnp.concatenate([bk_ref[0], tk_ref[...], kv_ref[:count]], axis=0)
+    width = heads * rows
+    dk = jnp.zeros((own + count, HEAD_WIDTH), jnp.float32)
+    dv = jnp.zeros((own + count, HEAD_WIDTH), jnp.float32)
+    for chunk in range(q_ref.shape[2] // (heads * HEAD_WIDTH)):
+        at = slice(chunk * width, (chunk + 1) * width)
+        q = stacked(q_ref, chunk, heads)
+        g = stacked(g_ref, chunk, heads)
+        factor = factor_ref[0:1, at]
+        w = (e_ref[:, at] * factor).astype(jnp.bfloat16)
+        ds = (gs_ref[:, at] * factor).astype(jnp.bfloat16)
+        dk += mm(ds, q)
+        dv += mm(w, g)
+        dq = mm(keys, jnp.concatenate([ds, ds_ref[:, at]], axis=0), TN) * scale
+        for j in range(heads):
+            head = chunk * heads + j
+            dq_ref[0, :, head * HEAD_WIDTH : (head + 1) * HEAD_WIDTH] = (
+                dq[:, j * rows : (j + 1) * rows].T.astype(jnp.bfloat16)
+            )
+    dk = (dk * scale).astype(jnp.bfloat16)
+    dv = dv.astype(jnp.bfloat16)
+    branch_ref[0, :, :HEAD_WIDTH] = dk[:own]
+    branch_ref[0, :, HEAD_WIDTH:] = dv[:own]
+    trunk_ref[:, :HEAD_WIDTH] = dk[own:]
+    trunk_ref[:, HEAD_WIDTH:] = dv[own:]
+
+
+def call(kernel, out_shape, in_specs, flops, bytes_accessed):
+    return pl.pallas_call(
+        kernel,
+        out_shape=out_shape,
+        in_specs=in_specs,
+        out_specs=[VMEM] * len(out_shape),
+        cost_estimate=pl.CostEstimate(
+            flops=flops, bytes_accessed=bytes_accessed, transcendentals=0
+        ),
+        compiler_params=pltpu.CompilerParams(vmem_limit_bytes=16 << 20),
+    )
+
+
+def halved(rows, axis, bit):
+    size = lax.axis_size(axis)
+    mine = (lax.axis_index(axis) // bit) % 2
+    parts = rows.reshape(2, rows.shape[0] // 2, rows.shape[1])
+    other = lax.ppermute(
+        lax.dynamic_index_in_dim(parts, 1 - mine, 0, False),
+        axis,
+        [(i, i ^ bit) for i in range(size)],
+    )
+    kept = lax.dynamic_index_in_dim(parts, mine, 0, False)
+    return (kept.astype(jnp.float32) + other.astype(jnp.float32)).astype(jnp.bfloat16)
+
+
+def paired_shards(
+    queries,
+    branch_keys,
+    branch_value_rows,
+    trunk_key_rows,
+    trunk_value_rows,
+    attn_out,
+    out_grad,
+    block_mask,
+):
+    rows = queries.shape[1]
+    group = queries.shape[2] // HEAD_WIDTH
+    own = branch_keys.shape[1]
+    count = trunk_key_rows.shape[0]
+    trunk_blocks = block_mask.shape[2] - rows // BLK
+    heads = 2 if group % 2 == 0 else 1
+    lanes = group * rows
+    swap = [(0, 1), (1, 0)]
+    near_part = lax.axis_index("ctx").astype(jnp.int32).reshape(1)
+    far_part = 1 - near_part
+    far = lax.ppermute(jnp.concatenate([trunk_key_rows, trunk_value_rows], axis=0), "ctx", swap)
+    near = own + count
+    mac = 2 * lanes * HEAD_WIDTH
+    shape = jax.ShapeDtypeStruct
+    e, gs, stats = call(
+        functools.partial(own_kernel, trunk_blocks, heads),
+        [
+            shape((near, lanes), jnp.float32),
+            shape((near, lanes), jnp.float32),
+            shape((24, lanes), jnp.float32),
+        ],
+        [SMEM, SMEM] + [VMEM] * 7,
+        2 * near * mac,
+        6 * rows * lanes,
+    )(
+        block_mask,
+        near_part,
+        queries,
+        out_grad,
+        attn_out,
+        branch_keys,
+        branch_value_rows,
+        trunk_key_rows,
+        trunk_value_rows,
+    )
+    pair, ds, factor = call(
+        functools.partial(far_kernel, trunk_blocks, heads),
+        [
+            shape((count, 2 * HEAD_WIDTH), jnp.bfloat16),
+            shape((count, lanes), jnp.bfloat16),
+            shape((8, lanes), jnp.float32),
+        ],
+        [SMEM, SMEM] + [VMEM] * 4,
+        4 * count * mac,
+        4 * rows * lanes,
+    )(block_mask, far_part, queries, out_grad, far, stats)
+    came = lax.ppermute(pair, "ctx", swap)
+    query_out, branch_out, kept = call(
+        functools.partial(rest_kernel, heads),
+        [
+            shape(queries.shape, jnp.bfloat16),
+            shape((1, own, 2 * HEAD_WIDTH), jnp.bfloat16),
+            shape((count, 2 * HEAD_WIDTH), jnp.bfloat16),
+        ],
+        [VMEM] * 9,
+        (2 * near + near + count) * mac,
+        6 * rows * lanes,
+    )(queries, out_grad, branch_keys, trunk_key_rows, far, e, gs, ds, factor)
+    total = (kept.astype(jnp.float32) + came.astype(jnp.float32)).astype(jnp.bfloat16)
+    bit = lax.axis_size("branch") // 2
+    while bit:
+        total = halved(total, "branch", bit)
+        bit //= 2
+    return (query_out, branch_out, total)
 
 
 def head_scores(query_row_block, key_row_block, score_scale):
@@ -19,8 +287,6 @@
         )
         * score_scale
     )
-
-
 def block_gradients(
     query_row_block,
     gradient_rows,
@@ -178,8 +444,22 @@
 
 
 def solution(mesh):
+    ctx, branch = mesh.shape["ctx"], mesh.shape["branch"]
+
+    def body(queries, *rest):
+        trunk_part = rest[2].shape[0]
+        paired = (
+            ctx == 2
+            and branch & (branch - 1) == 0
+            and queries.shape[0] == 1
+            and queries.shape[1] == BLK
+            and trunk_part % (8 * branch) == 0
+            and trunk_part <= 1024
+        )
+        return (paired_shards if paired else shards)(queries, *rest)
+
     return jax.shard_map(
-        shards,
+        body,
         mesh=mesh,
         in_specs=(
             P(("ctx", "branch"), None, "head"),

time: 79.8 us -> 25.3 us (0.32)
  waiting for transfers between devices: 31.9 us -> 6.93 us
  between operations: 14.9 us -> 0.77 us
  blocking collectives: 10.2 us -> 0 us
  starting transfers between devices: 0.08 us -> 7.36 us
  matrix products: 5.74 us -> 0 us
  local copies, waits for them, and re-layouts: 9.88 us -> 4.29 us
  other arithmetic: 6.35 us -> 1.44 us
  Pallas kernels: 0 us -> 4.11 us
    reduce_scatter x2 -> x0, waiting for transfers between devices: 31.9 us -> none  [the longest x1 20.5 us: shards(): lax.psum_scatter(reduced, 'branch', scatter_dimension=0, tiled=True)]
    all_gather x2 -> x0, blocking collectives: 10.2 us -> none  [the longest x1 5.73 us: shards(): lax.all_gather(trunk_key_rows, 'ctx', axis=0, tiled=True)]
    ppermute x0 -> x4, starting transfers between devices: none -> 7.36 us  [the longest x2 4.29 us: halved(): lax.ppermute(lax.dynamic_index_in_dim(parts, 1 - mine, 0, False), axis, [...]
    ppermute x0 -> x4, waiting for transfers between devices: none -> 6.93 us  [the longest x2 4.26 us: halved(): lax.ppermute(lax.dynamic_index_in_dim(parts, 1 - mine, 0, False), axis, [...]
    dot_general x29 -> x0, matrix products: 5.74 us -> none  [the longest x7 1.54 us: head_scores(): jnp.einsum('igd,kd->gik', query_row_block, key_row_block, preferred_eleme...]
    pallas_call x0 -> x3, Pallas kernels: none -> 4.11 us  [the longest x1 1.53 us: paired_shards(): call(functools.partial(far_kernel, trunk_blocks, heads), [shape((count, 2...]
    select_n x7 -> x0, other arithmetic: 3.93 us -> none  [the longest x6 3.92 us: trunk_allowed(): onehot = (tokens[None, :] // BLK == blocks[:, None]).astype(jnp.float32)]
    dynamic_slice x6 -> x0, local copies, waits for them, and re-layouts: 3.52 us -> none  [shards(): lax.scan(stats_step, (row_max, row_total), (key_blocks, offsets))]
  transfers between devices with their start and end apart: 2 -> 4, of which waited for: 2 -> 3; matrix products, arithmetic and copies ran while one was open for 3% -> 0% of each run, Pallas kernels for 0% -> 10%
where the time goes in v1:
time: 25.3 us; the launch traced here: 24.9 us
  starting transfers between devices  7.36 us (29%)
  waiting for transfers between devices  6.93 us (27%)
  local copies, waits for them, and re-layouts  4.29 us (17%)
  Pallas kernels  4.11 us (16%)
  other arithmetic  1.44 us (6%)
  between operations  0.77 us (3%)
    ppermute x2, starting transfers between devices, halved(): lax.ppermute(lax.dynamic_index_in_dim(parts, 1 - mine, 0, False), axis, [...  4.29 us
    unnamed x20, local copies, waits for them, and re-layouts  4.27 us
    ppermute x2, waiting for transfers between devices, halved(): lax.ppermute(lax.dynamic_index_in_dim(parts, 1 - mine, 0, False), axis, [...  4.26 us
    ppermute x1, starting transfers between devices, paired_shards(): lax.ppermute(jnp.concatenate([trunk_key_rows, trunk_value_rows], axis=0),...  3 us
    ppermute x1, waiting for transfers between devices, paired_shards(): came = lax.ppermute(pair, 'ctx', swap)  2.67 us
    pallas_call x1, Pallas kernels, paired_shards(): call(functools.partial(far_kernel, trunk_blocks, heads), [shape((count, 2...  1.53 us
    pallas_call x1, Pallas kernels, paired_shards(): call(functools.partial(rest_kernel, heads), [shape(queries.shape, jnp.bfl...  1.37 us
    pallas_call x1, Pallas kernels, paired_shards(): call(functools.partial(own_kernel, trunk_blocks, heads), [shape((near, la...  1.21 us
  transfers between devices with their start and end apart: 4, of which 3 were waited for; matrix products, arithmetic and copies ran while one was open for 0% of the time, Pallas kernels for 10%

profile of v1, /device:TPU:0, one launch (start us, length us, event | category | flops | bytes accessed | tf_op | source)
XLA Modules:
  0.0 24.9 jit_solution(2131095438691801990)
XLA Ops:
  0.6 0.0 copy-start.6
  0.6 0.0 copy-start.5
  0.7 0.0 copy-start.7
  0.7 0.8 %pad_maximum_fusion = bf16[192,128]{1,0:T(8,128)(2,1)S(1)} fusion(bf16[96,128]{1,0:T(8,128)(2,1)} %tv_ref.1, bf16[96,128]{1,0:T(8,128)(2,1)} %tk_ref.3), kind=kLoop, calls=%fused_computation.1 | loop fusion | flops 98304 | bytes 98304 | tf_op jit(solution)/shard_map/concatenate | solution.py:227
  1.5 3.0 %collective-permute-start = (bf16[192,128]{1,0:T(8,128)(2,1)S(1)}, bf16[192,128]{1,0:T(8,128)(2,1)S(1)}, u32[]{:S(2)}, u32[]{:S(2)}) collective-permute-start(bf16[192,128]{1,0:T(8,128)(2,1)S(1)} %pad_maximum_fusion), channel_id=1, source_target_pairs={{0,16},{16,0},{1,17},{17,1},{2,18},{18,2},{3,19},{19,3},{4,20},{20... | collective-permute-start | bytes 147464 | tf_op jit(solution)/shard_map/ppermute | solution.py:227
  4.5 0.0 copy-start.9
  4.5 0.0 copy-done.6
  4.5 0.0 copy-done.5
  4.5 0.0 copy-done.7
  4.5 0.6 %copy-done.9 = s32[1,1,3]{2,1,0:T(1,128)S(1)} copy-done((s32[1,1,3]{2,1,0:T(1,128)S(1)}, s32[1,1,3]{2,1,0:T(1,128)}, u32[]{:S(2)}) %copy-start.9) | copy-done | bytes 36
  5.1 0.0 copy-start
  5.1 0.9 %copy-done = bf16[1,128,1024]{2,1,0:T(8,128)(2,1)S(1)} copy-done((bf16[1,128,1024]{2,1,0:T(8,128)(2,1)S(1)}, bf16[1,128,1024]{2,1,0:T(8,128)(2,1)}, u32[]{:S(2)}) %copy-start) | copy-done | bytes 262168
  6.1 0.0 copy-start.2
  6.1 0.9 %copy-done.2 = bf16[1,128,1024]{2,1,0:T(8,128)(2,1)S(1)} copy-done((bf16[1,128,1024]{2,1,0:T(8,128)(2,1)S(1)}, bf16[1,128,1024]{2,1,0:T(8,128)(2,1)}, u32[]{:S(2)}) %copy-start.2) | copy-done | bytes 262168
  7.0 0.0 copy-start.4
  7.0 0.9 %copy-done.4 = bf16[1,128,1024]{2,1,0:T(8,128)(2,1)S(1)} copy-done((bf16[1,128,1024]{2,1,0:T(8,128)(2,1)S(1)}, bf16[1,128,1024]{2,1,0:T(8,128)(2,1)}, u32[]{:S(2)}) %copy-start.4) | copy-done | bytes 262168
  8.0 0.0 copy-start.8
  8.0 0.8 %copy-done.8 = bf16[1,128,128]{2,1,0:T(8,128)(2,1)S(1)} copy-done((bf16[1,128,128]{2,1,0:T(8,128)(2,1)S(1)}, bf16[1,128,128]{2,1,0:T(8,128)(2,1)}, u32[]{:S(2)}) %copy-start.8) | copy-done | bytes 32792
  8.7 0.0 copy-start.1
  8.7 0.0 copy-start.3
  8.7 1.2 %shard_map.103 = (f32[224,1024]{1,0:T(8,128)S(1)}, f32[224,1024]{1,0:T(8,128)S(1)}, f32[24,1024]{1,0:T(8,128)S(1)}) custom-call(s32[1,1,3]{2,1,0:T(1,128)S(1)} %copy-done.9, s32[1]{0:T(128)} %bitcast.part_ref, bf16[1,128,1024]{2,1,0:T(8,128)(2,1)S(1)} %copy-done, bf16[1,128,1024]{2,1,0:T(8,128)(2,1)S(1)} %copy-done.2, bf16[1,128,1024]{2,1,0:T(8,128)(2,1)S(1)} %copy-done.4, ...), custom_call_target="tpu_custom_call" | custom-call | flops 117440512 | bytes 786432 | tf_op jit(solution)/shard_map/pallas_call | solution.py:231
  9.9 0.0 collective-permute-done.kv_ref
  10.0 0.0 copy-done.1
  10.0 0.0 copy-done.3
  10.0 1.5 %shard_map.104 = (bf16[96,256]{1,0:T(8,128)(2,1)S(1)}, bf16[96,1024]{1,0:T(8,128)(2,1)S(1)}, f32[8,1024]{1,0:T(8,128)S(1)}) custom-call(s32[1,1,3]{2,1,0:T(1,128)S(1)} %copy-done.9, s32[1]{0:T(128)S(6)} %sub.14.part_ref, bf16[1,128,1024]{2,1,0:T(8,128)(2,1)S(1)} %copy-done.1, bf16[1,128,1024]{2,1,0:T(8,128)(2,1)S(1)} %copy-done.3, ...), custom_call_target="tpu_custom_call" | custom-call | flops 100663296 | bytes 524288 | tf_op jit(solution)/shard_map/pallas_call | solution.py:252
  11.5 0.1 collective-permute-start.1
  11.6 1.4 %shard_map.105 = (bf16[1,128,1024]{2,1,0:T(8,128)(2,1)}, bf16[1,128,256]{2,1,0:T(8,128)(2,1)}, bf16[96,256]{1,0:T(8,128)(2,1)S(1)}) custom-call(bf16[1,128,1024]{2,1,0:T(8,128)(2,1)S(1)} %copy-done.1, bf16[1,128,1024]{2,1,0:T(8,128)(2,1)S(1)} %copy-done.3, bf16[1,128,128]{2,1,0:T(8,128)(2,1)S(1)} %copy-done.6, bf16[96,128]{1,0:T(8,128)(2,1)S(1)} %copy-done.5, ...), custom_call_target="tpu_custom_call" | custom-call | flops 201326592 | bytes 786432 | tf_op jit(solution)/shard_map/pallas_call | solution.py:264
  13.0 2.7 %collective-permute-done.1 = bf16[96,256]{1,0:T(8,128)(2,1)S(1)} collective-permute-done((bf16[96,256]{1,0:T(8,128)(2,1)S(1)}, bf16[96,256]{1,0:T(8,128)(2,1)S(1)}, u32[]{:S(2)}, u32[]{:S(2)}) %collective-permute-start.1) | collective-permute-done | bytes 49184 | tf_op jit(solution)/shard_map/ppermute | solution.py:263
  15.7 2.7 %collective-permute-start.2 = (bf16[48,256]{1,0:T(8,128)(2,1)S(1)}, bf16[48,256]{1,0:T(8,128)(2,1)S(1)}, u32[]{:S(2)}, u32[]{:S(2)}) collective-permute-start(bf16[48,256]{1,0:T(8,128)(2,1)S(1)} %dynamic-slice_bitcast_fusion), channel_id=1, source_target_pairs={{0,8},{4,12},{8,0},{12,4},{1,9},{5,13},{9,1},{13,5},{2,10},{6,14},... | collective-permute-start | bytes 73736 | tf_op jit(solution)/shard_map/ppermute | solution.py:198
  18.4 2.1 %collective-permute-done.2 = bf16[48,256]{1,0:T(8,128)(2,1)S(1)} collective-permute-done((bf16[48,256]{1,0:T(8,128)(2,1)S(1)}, bf16[48,256]{1,0:T(8,128)(2,1)S(1)}, u32[]{:S(2)}, u32[]{:S(2)}) %collective-permute-start.2) | collective-permute-done | bytes 24608 | tf_op jit(solution)/shard_map/ppermute | solution.py:198
  20.5 1.6 %collective-permute-start.3 = (bf16[24,256]{1,0:T(8,128)(2,1)S(1)}, bf16[24,256]{1,0:T(8,128)(2,1)S(1)}, u32[]{:S(2)}, u32[]{:S(2)}) collective-permute-start(bf16[24,256]{1,0:T(8,128)(2,1)S(1)} %dynamic-slice_bitcast_fusion.1), channel_id=1, source_target_pairs={{0,4},{4,0},{8,12},{12,8},{1,5},{5,1},{9,13},{13,9},{2,6},{6,2},{1... | collective-permute-start | bytes 36872 | tf_op jit(solution)/shard_map/ppermute | solution.py:198
  22.2 2.1 %collective-permute-done.3 = bf16[24,256]{1,0:T(8,128)(2,1)S(1)} collective-permute-done((bf16[24,256]{1,0:T(8,128)(2,1)S(1)}, bf16[24,256]{1,0:T(8,128)(2,1)S(1)}, u32[]{:S(2)}, u32[]{:S(2)}) %collective-permute-start.3) | collective-permute-done | bytes 12320 | tf_op jit(solution)/shard_map/ppermute | solution.py:198
  24.3 0.6 %fusion.1 = bf16[24,256]{1,0:T(8,128)(2,1)} fusion(bf16[24,256]{1,0:T(8,128)(2,1)S(1)} %collective-permute-done.3, bf16[2,24,256]{2,1,0:T(8,128)(2,1)S(1)} %bitcast.16, s32[]{:T(128)S(6)} %select_n.35), kind=kLoop, calls=%fused_computation.5 | loop fusion | flops 24576 | bytes 36868 | tf_op jit(solution)/shard_map/convert_element_type | solution.py:204
  (4 shorter events, 0.0 us)
Async XLA Ops:
  0.6 3.8 %copy-start.6 = (bf16[1,128,128]{2,1,0:T(8,128)(2,1)S(1)}, bf16[1,128,128]{2,1,0:T(8,128)(2,1)}, u32[]{:S(2)}) copy-start(bf16[1,128,128]{2,1,0:T(8,128)(2,1)} %bk_ref.3) | copy-start | bytes 98308
  0.6 3.8 %copy-start.5 = (bf16[96,128]{1,0:T(8,128)(2,1)S(1)}, bf16[96,128]{1,0:T(8,128)(2,1)}, u32[]{:S(2)}) copy-start(bf16[96,128]{1,0:T(8,128)(2,1)} %tk_ref.3) | copy-start | bytes 73732
  0.7 3.8 %copy-start.7 = (bf16[96,128]{1,0:T(8,128)(2,1)S(1)}, bf16[96,128]{1,0:T(8,128)(2,1)}, u32[]{:S(2)}) copy-start(bf16[96,128]{1,0:T(8,128)(2,1)} %tv_ref.1) | copy-start | bytes 73732
  1.5 8.5 %collective-permute-start = (bf16[192,128]{1,0:T(8,128)(2,1)S(1)}, bf16[192,128]{1,0:T(8,128)(2,1)S(1)}, u32[]{:S(2)}, u32[]{:S(2)}) collective-permute-start(bf16[192,128]{1,0:T(8,128)(2,1)S(1)} %pad_maximum_fusion), channel_id=1, source_target_pairs={{0,16},{16,0},{1,17},{17,1},{2,18},{18,2},{3,19},{19,3},{4,20},{20... | collective-permute-start | bytes 147464 | tf_op jit(solution)/shard_map/ppermute | solution.py:227
  4.5 0.7 %copy-start.9 = (s32[1,1,3]{2,1,0:T(1,128)S(1)}, s32[1,1,3]{2,1,0:T(1,128)}, u32[]{:S(2)}) copy-start(s32[1,1,3]{2,1,0:T(1,128)} %mask_ref.3) | copy-start | bytes 40
  5.1 0.9 %copy-start = (bf16[1,128,1024]{2,1,0:T(8,128)(2,1)S(1)}, bf16[1,128,1024]{2,1,0:T(8,128)(2,1)}, u32[]{:S(2)}) copy-start(bf16[1,128,1024]{2,1,0:T(8,128)(2,1)} %q_ref.5) | copy-start | bytes 786436
  6.1 0.9 %copy-start.2 = (bf16[1,128,1024]{2,1,0:T(8,128)(2,1)S(1)}, bf16[1,128,1024]{2,1,0:T(8,128)(2,1)}, u32[]{:S(2)}) copy-start(bf16[1,128,1024]{2,1,0:T(8,128)(2,1)} %g_ref.5) | copy-start | bytes 786436
  7.0 0.9 %copy-start.4 = (bf16[1,128,1024]{2,1,0:T(8,128)(2,1)S(1)}, bf16[1,128,1024]{2,1,0:T(8,128)(2,1)}, u32[]{:S(2)}) copy-start(bf16[1,128,1024]{2,1,0:T(8,128)(2,1)} %o_ref.1) | copy-start | bytes 786436
  8.0 0.8 %copy-start.8 = (bf16[1,128,128]{2,1,0:T(8,128)(2,1)S(1)}, bf16[1,128,128]{2,1,0:T(8,128)(2,1)}, u32[]{:S(2)}) copy-start(bf16[1,128,128]{2,1,0:T(8,128)(2,1)} %bv_ref.1) | copy-start | bytes 98308
  8.7 1.2 %copy-start.1 = (bf16[1,128,1024]{2,1,0:T(8,128)(2,1)S(1)}, bf16[1,128,1024]{2,1,0:T(8,128)(2,1)}, u32[]{:S(2)}) copy-start(bf16[1,128,1024]{2,1,0:T(8,128)(2,1)} %q_ref.5) | copy-start | bytes 786436
  8.7 1.2 %copy-start.3 = (bf16[1,128,1024]{2,1,0:T(8,128)(2,1)S(1)}, bf16[1,128,1024]{2,1,0:T(8,128)(2,1)}, u32[]{:S(2)}) copy-start(bf16[1,128,1024]{2,1,0:T(8,128)(2,1)} %g_ref.5) | copy-start | bytes 786436
  11.5 4.2 %collective-permute-start.1 = (bf16[96,256]{1,0:T(8,128)(2,1)S(1)}, bf16[96,256]{1,0:T(8,128)(2,1)S(1)}, u32[]{:S(2)}, u32[]{:S(2)}) collective-permute-start(bf16[96,256]{1,0:T(8,128)(2,1)S(1)} %get-tuple-element.20), channel_id=1, source_target_pairs={{0,16},{16,0},{1,17},{17,1},{2,18},{18,2},{3,19},{19,3},{4,20},{20... | collective-permute-start | bytes 147464 | tf_op jit(solution)/shard_map/ppermute | solution.py:263
  15.7 4.8 %collective-permute-start.2 = (bf16[48,256]{1,0:T(8,128)(2,1)S(1)}, bf16[48,256]{1,0:T(8,128)(2,1)S(1)}, u32[]{:S(2)}, u32[]{:S(2)}) collective-permute-start(bf16[48,256]{1,0:T(8,128)(2,1)S(1)} %dynamic-slice_bitcast_fusion), channel_id=1, source_target_pairs={{0,8},{4,12},{8,0},{12,4},{1,9},{5,13},{9,1},{13,5},{2,10},{6,14},... | collective-permute-start | bytes 73736 | tf_op jit(solution)/shard_map/ppermute | solution.py:198
  20.5 3.8 %collective-permute-start.3 = (bf16[24,256]{1,0:T(8,128)(2,1)S(1)}, bf16[24,256]{1,0:T(8,128)(2,1)S(1)}, u32[]{:S(2)}, u32[]{:S(2)}) collective-permute-start(bf16[24,256]{1,0:T(8,128)(2,1)S(1)} %dynamic-slice_bitcast_fusion.1), channel_id=1, source_target_pairs={{0,4},{4,0},{8,12},{12,8},{1,5},{5,1},{9,13},{13,9},{2,6},{6,2},{1... | collective-permute-start | bytes 36872 | tf_op jit(solution)/shard_map/ppermute | solution.py:198

commit v2 on v1

--- a/solution.py
+++ b/solution.py
@@ -14,7 +14,9 @@
 
 masked_fill = -1e30
 VMEM = pl.BlockSpec(memory_space=pltpu.VMEM)
+HBM = pl.BlockSpec(memory_space=pltpu.HBM)
 SMEM = pl.BlockSpec(memory_space=pltpu.SMEM)
+LOG2_E = 1.4426950408889634
 NT = (((1,), (1,)), ((), ()))
 TN = (((0,), (0,)), ((), ()))
 
@@ -33,70 +35,110 @@
     )
 
 
-def trunk_visible(mask_ref, part_ref, shape, trunk_blocks):
-    token = part_ref[0] * shape[0] + lax.broadcasted_iota(jnp.int32, shape, 0)
+def trunk_bias(mask_ref, part, shape, trunk_blocks):
+    token = part * shape[0] + lax.broadcasted_iota(jnp.int32, shape, 0)
     visible = jnp.zeros(shape, jnp.int32)
     for block in range(trunk_blocks):
         inside = (token >= block * BLK) & (token < (block + 1) * BLK)
         visible = jnp.where(inside, mask_ref[0, 0, block], visible)
-    return visible > 0
+    return jnp.where(visible > 0, 0.0, masked_fill)
+
+
+def pack_kernel(tk_ref, tv_ref, kv_ref, sems):
+    count = tk_ref.shape[0]
+    copies = [
+        pltpu.make_async_copy(tk_ref, kv_ref.at[:count], sems.at[0]),
+        pltpu.make_async_copy(tv_ref, kv_ref.at[count:], sems.at[1]),
+    ]
+    for copy in copies:
+        copy.start()
+    for copy in copies:
+        copy.wait()
 
 
 def own_kernel(
     trunk_blocks,
     heads,
-    mask_ref,
     part_ref,
+    mask_in,
+    q_in,
+    g_in,
+    o_in,
+    bk_in,
+    bv_in,
+    tk_in,
+    tv_in,
     q_ref,
     g_ref,
-    o_ref,
-    bk_ref,
-    bv_ref,
-    tk_ref,
-    tv_ref,
+    keys_ref,
     e_ref,
     gs_ref,
     stat_ref,
+    bias_ref,
+    o_ref,
+    values_ref,
+    mask_ref,
+    sems,
 ):
     rows = q_ref.shape[1]
-    own = bk_ref.shape[1]
-    scale = 1.0 / math.sqrt(HEAD_WIDTH)
-    keys = jnp.concatenate([bk_ref[0], tk_ref[...]], axis=0)
-    values = jnp.concatenate([bv_ref[0], tv_ref[...]], axis=0)
+    own = bk_in.shape[1]
+    count = tk_in.shape[0]
     width = heads * rows
+    scale = LOG2_E / math.sqrt(HEAD_WIDTH)
+    chunks = q_ref.shape[2] // (heads * HEAD_WIDTH)
+    pairs = [
+        (mask_in, mask_ref),
+        (bk_in.at[0], keys_ref.at[:own]),
+        (tk_in, keys_ref.at[own:]),
+        (q_in, q_ref),
+        (bv_in.at[0], values_ref.at[:own]),
+        (tv_in, values_ref.at[own:]),
+        (g_in, g_ref),
+        (o_in, o_ref),
+    ]
+    copies = [pltpu.make_async_copy(a, b, sems.at[i]) for i, (a, b) in enumerate(pairs)]
+    for copy in copies:
+        copy.start()
     key_row = lax.broadcasted_iota(jnp.int32, (own, rows), 0)
     query_row = lax.broadcasted_iota(jnp.int32, (own, rows), 1)
-    causal = key_row <= query_row
-    visible = trunk_visible(mask_ref, part_ref, (tk_ref.shape[0], rows), trunk_blocks)
-    allowed = jnp.concatenate([jnp.concatenate([causal, visible], axis=0)] * heads, axis=1)
+    causal = jnp.where(key_row <= query_row, 0.0, masked_fill)
     ones = jnp.ones((8, HEAD_WIDTH), jnp.bfloat16)
-    for chunk in range(q_ref.shape[2] // (heads * HEAD_WIDTH)):
+    for copy in copies[:4]:
+        copy.wait()
+    bias_ref[...] = trunk_bias(mask_ref, 1 - part_ref[0], (count, rows), trunk_blocks)
+    bias = trunk_bias(mask_ref, part_ref[0], (count, rows), trunk_blocks)
+    bias = jnp.concatenate([jnp.concatenate([causal, bias], axis=0)] * heads, axis=1)
+    keys = keys_ref[...]
+    for chunk in range(chunks):
         at = slice(chunk * width, (chunk + 1) * width)
         q = stacked(q_ref, chunk, heads)
+        s = mm(keys, q, NT) * scale + bias
+        top = jnp.max(s, axis=0, keepdims=True)
+        e = jnp.exp2(s - top)
+        e_ref[:, at] = e
+        stat_ref[0:8, at] = jnp.broadcast_to(top, (8, width))
+        stat_ref[8:16, at] = jnp.broadcast_to(jnp.sum(e, axis=0, keepdims=True), (8, width))
+    for copy in copies[4:]:
+        copy.wait()
+    values = values_ref[...]
+    for chunk in range(chunks):
+        at = slice(chunk * width, (chunk + 1) * width)
         g = stacked(g_ref, chunk, heads)
         prod = g.astype(jnp.float32) * stacked(o_ref, chunk, heads).astype(jnp.float32)
         high = prod.astype(jnp.bfloat16)
         low = (prod - high.astype(jnp.float32)).astype(jnp.bfloat16)
         dot = mm(ones, high, NT) + mm(ones, low, NT)
-        s = jnp.where(allowed, mm(keys, q, NT) * scale, masked_fill)
-        top = jnp.max(s, axis=0, keepdims=True)
-        e = jnp.exp(s - top)
-        e_ref[:, at] = e
-        gs_ref[:, at] = e * (mm(values, g, NT) - dot[:1])
-        stat_ref[0:8, at] = jnp.broadcast_to(top, (8, width))
-        stat_ref[8:16, at] = jnp.broadcast_to(jnp.sum(e, axis=0, keepdims=True), (8, width))
+        gs_ref[:, at] = e_ref[:, at] * (mm(values, g, NT) - dot[:1])
         stat_ref[16:24, at] = dot
 
 
 def far_kernel(
-    trunk_blocks,
     heads,
-    mask_ref,
-    part_ref,
     q_ref,
     g_ref,
     kv_ref,
     stat_ref,
+    bias_ref,
     pair_ref,
     ds_ref,
     factor_ref,
@@ -107,19 +149,18 @@
     keys = kv_ref[:count]
     values = kv_ref[count:]
     width = heads * rows
-    visible = trunk_visible(mask_ref, part_ref, (count, rows), trunk_blocks)
-    visible = jnp.concatenate([visible] * heads, axis=1)
+    bias = jnp.concatenate([bias_ref[...]] * heads, axis=1)
     dk = jnp.zeros((count, HEAD_WIDTH), jnp.float32)
     dv = jnp.zeros((count, HEAD_WIDTH), jnp.float32)
     for chunk in range(q_ref.shape[2] // (heads * HEAD_WIDTH)):
         at = slice(chunk * width, (chunk + 1) * width)
         q = stacked(q_ref, chunk, heads)
         g = stacked(g_ref, chunk, heads)
-        s = jnp.where(visible, mm(keys, q, NT) * scale, masked_fill)
+        s = mm(keys, q, NT) * (scale * LOG2_E) + bias
         old = stat_ref[0:1, at]
         top = jnp.maximum(old, jnp.max(s, axis=0, keepdims=True))
-        e = jnp.exp(s - top)
-        shrink = jnp.exp(old - top)
+        e = jnp.exp2(s - top)
+        shrink = jnp.exp2(old - top)
         total = stat_ref[8:9, at] * shrink + jnp.sum(e, axis=0, keepdims=True)
         inverse = 1.0 / total
         w = e * inverse
@@ -136,8 +177,7 @@
     heads,
     q_ref,
     g_ref,
-    bk_ref,
-    tk_ref,
+    near_ref,
     kv_ref,
     e_ref,
     gs_ref,
@@ -148,10 +188,10 @@
     trunk_ref,
 ):
     rows = q_ref.shape[1]
-    own = bk_ref.shape[1]
-    count = tk_ref.shape[0]
+    count = kv_ref.shape[0] // 2
+    own = near_ref.shape[0] - count
     scale = 1.0 / math.sqrt(HEAD_WIDTH)
-    keys = jnp.concatenate([bk_ref[0], tk_ref[...], kv_ref[:count]], axis=0)
+    keys = jnp.concatenate([near_ref[...], kv_ref[:count]], axis=0)
     width = heads * rows
     dk = jnp.zeros((own + count, HEAD_WIDTH), jnp.float32)
     dv = jnp.zeros((own + count, HEAD_WIDTH), jnp.float32)
@@ -178,12 +218,17 @@
     trunk_ref[:, HEAD_WIDTH:] = dv[own:]
 
 
-def call(kernel, out_shape, in_specs, flops, bytes_accessed):
+def in_hbm(*arrays):
+    return [pltpu.with_memory_space_constraint(array, pltpu.HBM) for array in arrays]
+
+
+def call(kernel, out_shape, in_specs, flops, bytes_accessed, scratch=()):
     return pl.pallas_call(
         kernel,
         out_shape=out_shape,
         in_specs=in_specs,
         out_specs=[VMEM] * len(out_shape),
+        scratch_shapes=scratch,
         cost_estimate=pl.CostEstimate(
             flops=flops, bytes_accessed=bytes_accessed, transcendentals=0
         ),
@@ -219,59 +264,77 @@
     own = branch_keys.shape[1]
     count = trunk_key_rows.shape[0]
     trunk_blocks = block_mask.shape[2] - rows // BLK
-    heads = 2 if group % 2 == 0 else 1
     lanes = group * rows
+    heads = group // 2 if group % 2 == 0 else group
     swap = [(0, 1), (1, 0)]
-    near_part = lax.axis_index("ctx").astype(jnp.int32).reshape(1)
-    far_part = 1 - near_part
-    far = lax.ppermute(jnp.concatenate([trunk_key_rows, trunk_value_rows], axis=0), "ctx", swap)
     near = own + count
     mac = 2 * lanes * HEAD_WIDTH
     shape = jax.ShapeDtypeStruct
-    e, gs, stats = call(
+    packed = call(
+        pack_kernel,
+        [shape((2 * count, HEAD_WIDTH), jnp.bfloat16)],
+        [HBM] * 2,
+        0,
+        8 * count * HEAD_WIDTH,
+        [pltpu.SemaphoreType.DMA((2,))],
+    )(*in_hbm(trunk_key_rows, trunk_value_rows))[0]
+    far = lax.ppermute(packed, "ctx", swap)
+    q, g, near_keys, e, gs, stats, bias = call(
         functools.partial(own_kernel, trunk_blocks, heads),
         [
+            shape(queries.shape, jnp.bfloat16),
+            shape(queries.shape, jnp.bfloat16),
+            shape((near, HEAD_WIDTH), jnp.bfloat16),
             shape((near, lanes), jnp.float32),
             shape((near, lanes), jnp.float32),
             shape((24, lanes), jnp.float32),
+            shape((count, rows), jnp.float32),
         ],
-        [SMEM, SMEM] + [VMEM] * 7,
+        [SMEM] + [HBM] * 8,
         2 * near * mac,
         6 * rows * lanes,
+        [
+            pltpu.VMEM(queries.shape, jnp.bfloat16),
+            pltpu.VMEM((near, HEAD_WIDTH), jnp.bfloat16),
+            pltpu.SMEM(block_mask.shape, jnp.int32),
+            pltpu.SemaphoreType.DMA((8,)),
+        ],
     )(
-        block_mask,
-        near_part,
-        queries,
-        out_grad,
-        attn_out,
-        branch_keys,
-        branch_value_rows,
-        trunk_key_rows,
-        trunk_value_rows,
+        lax.axis_index("ctx").astype(jnp.int32).reshape(1),
+        *in_hbm(
+            block_mask,
+            queries,
+            out_grad,
+            attn_out,
+            branch_keys,
+            branch_value_rows,
+            trunk_key_rows,
+            trunk_value_rows,
+        ),
     )
     pair, ds, factor = call(
-        functools.partial(far_kernel, trunk_blocks, heads),
+        functools.partial(far_kernel, group),
         [
             shape((count, 2 * HEAD_WIDTH), jnp.bfloat16),
             shape((count, lanes), jnp.bfloat16),
             shape((8, lanes), jnp.float32),
         ],
-        [SMEM, SMEM] + [VMEM] * 4,
+        [VMEM] * 5,
         4 * count * mac,
         4 * rows * lanes,
-    )(block_mask, far_part, queries, out_grad, far, stats)
+    )(q, g, far, stats, bias)
     came = lax.ppermute(pair, "ctx", swap)
     query_out, branch_out, kept = call(
-        functools.partial(rest_kernel, heads),
+        functools.partial(rest_kernel, group),
         [
             shape(queries.shape, jnp.bfloat16),
             shape((1, own, 2 * HEAD_WIDTH), jnp.bfloat16),
             shape((count, 2 * HEAD_WIDTH), jnp.bfloat16),
         ],
-        [VMEM] * 9,
-        (2 * near + near + count) * mac,
+        [VMEM] * 8,
+        (3 * near + count) * mac,
         6 * rows * lanes,
-    )(queries, out_grad, branch_keys, trunk_key_rows, far, e, gs, ds, factor)
+    )(q, g, near_keys, far, e, gs, ds, factor)
     total = (kept.astype(jnp.float32) + came.astype(jnp.float32)).astype(jnp.bfloat16)
     bit = lax.axis_size("branch") // 2
     while bit:

time: 25.3 us -> 21 us (0.83)
  local copies, waits for them, and re-layouts: 4.29 us -> 0.02 us
  starting transfers between devices: 7.36 us -> 10.2 us
  waiting for transfers between devices: 6.93 us -> 4.62 us
  other arithmetic: 1.44 us -> 0.63 us
  Pallas kernels: 4.11 us -> 4.72 us
    unnamed x20 -> x0, local copies, waits for them, and re-layouts: 4.27 us -> none
    ppermute x1, starting transfers between devices: 0.07 us -> 2.09 us  [paired_shards(): came = lax.ppermute(pair, 'ctx', swap)]
    ppermute x1, waiting for transfers between devices: 2.67 us -> 0.76 us  [paired_shards(): came = lax.ppermute(pair, 'ctx', swap)]
    concatenate x1 -> x0, other arithmetic: 0.81 us -> none  [paired_shards(): jnp.concatenate([trunk_key_rows, trunk_value_rows], axis=0)]
    ppermute x2, starting transfers between devices: 4.29 us -> 5.02 us  [halved(): lax.ppermute(lax.dynamic_index_in_dim(parts, 1 - mine, 0, False), axis, [...]
    pallas_call x3 -> x4, Pallas kernels: 4.11 us -> 4.72 us  [the longest x1 2.01 us: paired_shards(): call(functools.partial(own_kernel, trunk_blocks, heads), [shape(queries.s...]
    ppermute x2, waiting for transfers between devices: 4.26 us -> 3.8 us  [halved(): lax.ppermute(lax.dynamic_index_in_dim(parts, 1 - mine, 0, False), axis, [...]
  transfers between devices with their start and end apart: 4 -> 4, of which waited for: 3 -> 4; matrix products, arithmetic and copies ran while one was open for 0% -> 0% of each run, Pallas kernels for 10% -> 16%
where the time goes in v2:
time: 21 us; the launch traced here: 20.8 us
  starting transfers between devices  10.2 us (49%)
  Pallas kernels  4.72 us (22%)
  waiting for transfers between devices  4.62 us (22%)
  between operations  0.68 us (3%)
  other arithmetic  0.63 us (3%)
    ppermute x2, starting transfers between devices, halved(): lax.ppermute(lax.dynamic_index_in_dim(parts, 1 - mine, 0, False), axis, [...  5.02 us
    ppermute x2, waiting for transfers between devices, halved(): lax.ppermute(lax.dynamic_index_in_dim(parts, 1 - mine, 0, False), axis, [...  3.8 us
    ppermute x1, starting transfers between devices, paired_shards(): far = lax.ppermute(packed, 'ctx', swap)  3.06 us
    ppermute x1, starting transfers between devices, paired_shards(): came = lax.ppermute(pair, 'ctx', swap)  2.09 us
    pallas_call x1, Pallas kernels, paired_shards(): call(functools.partial(own_kernel, trunk_blocks, heads), [shape(queries.s...  2.01 us
    pallas_call x1, Pallas kernels, paired_shards(): call(functools.partial(rest_kernel, group), [shape(queries.shape, jnp.bfl...  1.3 us
    pallas_call x1, Pallas kernels, paired_shards(): call(pack_kernel, [shape((2 * count, HEAD_WIDTH), jnp.bfloat16)], [HBM] *...  0.78 us
    ppermute x1, waiting for transfers between devices, paired_shards(): came = lax.ppermute(pair, 'ctx', swap)  0.76 us
  transfers between devices with their start and end apart: 4, of which 4 were waited for; matrix products, arithmetic and copies ran while one was open for 0% of the time, Pallas kernels for 16%

profile of v2, /device:TPU:0, one launch (start us, length us, event | category | flops | bytes accessed | tf_op | source)
XLA Modules:
  0.0 20.8 jit_solution(11361057873596121646)
XLA Ops:
  0.6 0.8 %shard_map.104 = bf16[192,128]{1,0:T(8,128)(2,1)S(1)} custom-call(bf16[96,128]{1,0:T(8,128)(2,1)} %tk_ref.1, bf16[96,128]{1,0:T(8,128)(2,1)} %tv_ref.1), custom_call_target="tpu_custom_call" | custom-call | bytes 98304 | tf_op jit(solution)/shard_map/pallas_call | solution.py:273
  1.4 3.1 %collective-permute-start = (bf16[192,128]{1,0:T(8,128)(2,1)S(1)}, bf16[192,128]{1,0:T(8,128)(2,1)S(1)}, u32[]{:S(2)}, u32[]{:S(2)}) collective-permute-start(bf16[192,128]{1,0:T(8,128)(2,1)S(1)} %shard_map.104), channel_id=1, source_target_pairs={{0,16},{16,0},{1,17},{17,1},{2,18},{18,2},{3,19},{19,3},{4,20},{20... | collective-permute-start | bytes 147464 | tf_op jit(solution)/shard_map/ppermute | solution.py:281
  4.5 2.0 %shard_map.103 = (bf16[1,128,1024]{2,1,0:T(8,128)(2,1)S(1)}, bf16[1,128,1024]{2,1,0:T(8,128)(2,1)S(1)}, bf16[224,128]{1,0:T(8,128)(2,1)S(1)}, f32[224,1024]{1,0:...) custom-call(s32[1]{0:T(128)} %bitcast.part_ref, s32[1,1,3]{2,1,0:T(1,128)} %mask_in.1, ...), custom_call_target="tpu_custom_call" | custom-call | flops 117440512 | bytes 786432 | tf_op jit(solution)/shard_map/pallas_call | solution.py:282
  6.5 0.1 collective-permute-done.kv_ref
  6.5 0.6 %shard_map.105 = (bf16[96,256]{1,0:T(8,128)(2,1)S(1)}, bf16[96,1024]{1,0:T(8,128)(2,1)S(1)}, f32[8,1024]{1,0:T(8,128)S(1)}) custom-call(bf16[1,128,1024]{2,1,0:T(8,128)(2,1)S(1)} %get-tuple-element.16.q_ref, bf16[1,128,1024]{2,1,0:T(8,128)(2,1)S(1)} %get-tuple-element.17.g_ref, bf16[192,128]{1,0:T(8,128)(2,1)S(1)} %collective-permute-done.kv_ref, ...), custom_call_target="tpu_custom_call" | custom-call | flops 100663296 | bytes 524288 | tf_op jit(solution)/shard_map/pallas_call | solution.py:315
  7.2 2.1 %collective-permute-start.1 = (bf16[96,256]{1,0:T(8,128)(2,1)S(1)}, bf16[96,256]{1,0:T(8,128)(2,1)S(1)}, u32[]{:S(2)}, u32[]{:S(2)}) collective-permute-start(bf16[96,256]{1,0:T(8,128)(2,1)S(1)} %get-tuple-element.28), channel_id=1, source_target_pairs={{0,16},{16,0},{1,17},{17,1},{2,18},{18,2},{3,19},{19,3},{4,20},{20... | collective-permute-start | bytes 147464 | tf_op jit(solution)/shard_map/ppermute | solution.py:326
  9.3 1.3 %shard_map.106 = (bf16[1,128,1024]{2,1,0:T(8,128)(2,1)}, bf16[1,128,256]{2,1,0:T(8,128)(2,1)}, bf16[96,256]{1,0:T(8,128)(2,1)S(1)}) custom-call(bf16[1,128,1024]{2,1,0:T(8,128)(2,1)S(1)} %get-tuple-element.16.q_ref, bf16[1,128,1024]{2,1,0:T(8,128)(2,1)S(1)} %get-tuple-element.17.g_ref, bf16[224,128]{1,0:T(8,128)(2,1)S(1)} %get-tuple-element.18.near_ref, ...), custom_call_target="tpu_custom_call" | custom-call | flops 201326592 | bytes 786432 | tf_op jit(solution)/shard_map/pallas_call | solution.py:327
  10.6 0.8 %collective-permute-done.1 = bf16[96,256]{1,0:T(8,128)(2,1)S(1)} collective-permute-done((bf16[96,256]{1,0:T(8,128)(2,1)S(1)}, bf16[96,256]{1,0:T(8,128)(2,1)S(1)}, u32[]{:S(2)}, u32[]{:S(2)}) %collective-permute-start.1) | collective-permute-done | bytes 49184 | tf_op jit(solution)/shard_map/ppermute | solution.py:326
  11.4 3.2 %collective-permute-start.2 = (bf16[48,256]{1,0:T(8,128)(2,1)S(1)}, bf16[48,256]{1,0:T(8,128)(2,1)S(1)}, u32[]{:S(2)}, u32[]{:S(2)}) collective-permute-start(bf16[48,256]{1,0:T(8,128)(2,1)S(1)} %dynamic-slice_bitcast_fusion), channel_id=1, source_target_pairs={{0,8},{4,12},{8,0},{12,4},{1,9},{5,13},{9,1},{13,5},{2,10},{6,14},... | collective-permute-start | bytes 73736 | tf_op jit(solution)/shard_map/ppermute | solution.py:243
  14.5 1.9 %collective-permute-done.2 = bf16[48,256]{1,0:T(8,128)(2,1)S(1)} collective-permute-done((bf16[48,256]{1,0:T(8,128)(2,1)S(1)}, bf16[48,256]{1,0:T(8,128)(2,1)S(1)}, u32[]{:S(2)}, u32[]{:S(2)}) %collective-permute-start.2) | collective-permute-done | bytes 24608 | tf_op jit(solution)/shard_map/ppermute | solution.py:243
  16.5 1.9 %collective-permute-start.3 = (bf16[24,256]{1,0:T(8,128)(2,1)S(1)}, bf16[24,256]{1,0:T(8,128)(2,1)S(1)}, u32[]{:S(2)}, u32[]{:S(2)}) collective-permute-start(bf16[24,256]{1,0:T(8,128)(2,1)S(1)} %dynamic-slice_bitcast_fusion.1), channel_id=1, source_target_pairs={{0,4},{4,0},{8,12},{12,8},{1,5},{5,1},{9,13},{13,9},{2,6},{6,2},{1... | collective-permute-start | bytes 36872 | tf_op jit(solution)/shard_map/ppermute | solution.py:243
  18.3 1.9 %collective-permute-done.3 = bf16[24,256]{1,0:T(8,128)(2,1)S(1)} collective-permute-done((bf16[24,256]{1,0:T(8,128)(2,1)S(1)}, bf16[24,256]{1,0:T(8,128)(2,1)S(1)}, u32[]{:S(2)}, u32[]{:S(2)}) %collective-permute-start.3) | collective-permute-done | bytes 12320 | tf_op jit(solution)/shard_map/ppermute | solution.py:243
  20.2 0.6 %fusion.1 = bf16[24,256]{1,0:T(8,128)(2,1)} fusion(bf16[24,256]{1,0:T(8,128)(2,1)S(1)} %collective-permute-done.3, bf16[2,24,256]{2,1,0:T(8,128)(2,1)S(1)} %bitcast.16, s32[]{:T(128)S(6)} %select_n.35), kind=kLoop, calls=%fused_computation.4 | loop fusion | flops 24576 | bytes 36868 | tf_op jit(solution)/shard_map/convert_element_type | solution.py:249
  (4 shorter events, 0.0 us)
Async XLA Ops:
  1.4 5.1 %collective-permute-start = (bf16[192,128]{1,0:T(8,128)(2,1)S(1)}, bf16[192,128]{1,0:T(8,128)(2,1)S(1)}, u32[]{:S(2)}, u32[]{:S(2)}) collective-permute-start(bf16[192,128]{1,0:T(8,128)(2,1)S(1)} %shard_map.104), channel_id=1, source_target_pairs={{0,16},{16,0},{1,17},{17,1},{2,18},{18,2},{3,19},{19,3},{4,20},{20... | collective-permute-start | bytes 147464 | tf_op jit(solution)/shard_map/ppermute | solution.py:281
  7.2 4.2 %collective-permute-start.1 = (bf16[96,256]{1,0:T(8,128)(2,1)S(1)}, bf16[96,256]{1,0:T(8,128)(2,1)S(1)}, u32[]{:S(2)}, u32[]{:S(2)}) collective-permute-start(bf16[96,256]{1,0:T(8,128)(2,1)S(1)} %get-tuple-element.28), channel_id=1, source_target_pairs={{0,16},{16,0},{1,17},{17,1},{2,18},{18,2},{3,19},{19,3},{4,20},{20... | collective-permute-start | bytes 147464 | tf_op jit(solution)/shard_map/ppermute | solution.py:326
  11.4 5.1 %collective-permute-start.2 = (bf16[48,256]{1,0:T(8,128)(2,1)S(1)}, bf16[48,256]{1,0:T(8,128)(2,1)S(1)}, u32[]{:S(2)}, u32[]{:S(2)}) collective-permute-start(bf16[48,256]{1,0:T(8,128)(2,1)S(1)} %dynamic-slice_bitcast_fusion), channel_id=1, source_target_pairs={{0,8},{4,12},{8,0},{12,4},{1,9},{5,13},{9,1},{13,5},{2,10},{6,14},... | collective-permute-start | bytes 73736 | tf_op jit(solution)/shard_map/ppermute | solution.py:243
  16.5 3.8 %collective-permute-start.3 = (bf16[24,256]{1,0:T(8,128)(2,1)S(1)}, bf16[24,256]{1,0:T(8,128)(2,1)S(1)}, u32[]{:S(2)}, u32[]{:S(2)}) collective-permute-start(bf16[24,256]{1,0:T(8,128)(2,1)S(1)} %dynamic-slice_bitcast_fusion.1), channel_id=1, source_target_pairs={{0,4},{4,0},{8,12},{12,8},{1,5},{5,1},{9,13},{13,9},{2,6},{6,2},{1... | collective-permute-start | bytes 36872 | tf_op jit(solution)/shard_map/ppermute | solution.py:243

commit v3 on v2

--- a/solution.py
+++ b/solution.py
@@ -236,16 +236,22 @@
     )
 
 
-def halved(rows, axis, bit):
-    size = lax.axis_size(axis)
-    mine = (lax.axis_index(axis) // bit) % 2
+def halved(rows, bit, crossed):
+    size, heads = lax.axis_size("branch"), lax.axis_size("head")
+    mine = (lax.axis_index("branch") // bit) % 2
     parts = rows.reshape(2, rows.shape[0] // 2, rows.shape[1])
     other = lax.ppermute(
         lax.dynamic_index_in_dim(parts, 1 - mine, 0, False),
-        axis,
-        [(i, i ^ bit) for i in range(size)],
+        ("branch", "head"),
+        [
+            (i * heads + h, (i ^ bit) * heads + (h ^ crossed))
+            for i in range(size)
+            for h in range(heads)
+        ],
     )
     kept = lax.dynamic_index_in_dim(parts, mine, 0, False)
+    if crossed:
+        kept = lax.ppermute(kept, "head", [(h, h ^ 1) for h in range(heads)])
     return (kept.astype(jnp.float32) + other.astype(jnp.float32)).astype(jnp.bfloat16)
 
 
@@ -336,10 +342,10 @@
         6 * rows * lanes,
     )(q, g, near_keys, far, e, gs, ds, factor)
     total = (kept.astype(jnp.float32) + came.astype(jnp.float32)).astype(jnp.bfloat16)
-    bit = lax.axis_size("branch") // 2
-    while bit:
-        total = halved(total, "branch", bit)
-        bit //= 2
+    steps = lax.axis_size("branch").bit_length() - 1
+    crossings = steps // 2 * 2 if lax.axis_size("head") % 2 == 0 else 0
+    for step in range(steps):
+        total = halved(total, 1 << (steps - 1 - step), int(step < crossings))
     return (query_out, branch_out, total)
 
 

time: 21 us -> 19.7 us (0.938)
  waiting for transfers between devices: 4.62 us -> 2.78 us
  starting transfers between devices: 10.2 us -> 10.7 us
    ppermute x2 -> x4, waiting for transfers between devices: 3.8 us -> 1.96 us  [the longest x2 1.96 us: halved(): lax.ppermute(lax.dynamic_index_in_dim(parts, 1 - mine, 0, False), ('branc...]
    ppermute x2 -> x4, starting transfers between devices: 5.02 us -> 5.53 us  [the longest x2 3.04 us: halved(): kept = lax.ppermute(kept, 'head', [(h, h ^ 1) for h in range(heads)])]
  transfers between devices with their start and end apart: 4 -> 6, of which waited for: 4 -> 4; matrix products, arithmetic and copies ran while one was open for 0% -> 0% of each run, Pallas kernels for 16% -> 17%
where the time goes in v3:
time: 19.7 us; the launch traced here: 19.5 us
  starting transfers between devices  10.7 us (54%)
  Pallas kernels  4.72 us (24%)
  waiting for transfers between devices  2.78 us (14%)
  between operations  0.68 us (3%)
  other arithmetic  0.63 us (3%)
    ppermute x1, starting transfers between devices, paired_shards(): far = lax.ppermute(packed, 'ctx', swap)  3.06 us
    ppermute x2, starting transfers between devices, halved(): kept = lax.ppermute(kept, 'head', [(h, h ^ 1) for h in range(heads)])  3.04 us
    ppermute x2, starting transfers between devices, halved(): lax.ppermute(lax.dynamic_index_in_dim(parts, 1 - mine, 0, False), ('branc...  2.49 us
    ppermute x1, starting transfers between devices, paired_shards(): came = lax.ppermute(pair, 'ctx', swap)  2.09 us
    pallas_call x1, Pallas kernels, paired_shards(): call(functools.partial(own_kernel, trunk_blocks, heads), [shape(queries.s...  2.01 us
    ppermute x2, waiting for transfers between devices, halved(): lax.ppermute(lax.dynamic_index_in_dim(parts, 1 - mine, 0, False), ('branc...  1.96 us
    pallas_call x1, Pallas kernels, paired_shards(): call(functools.partial(rest_kernel, group), [shape(queries.shape, jnp.bfl...  1.3 us
    pallas_call x1, Pallas kernels, paired_shards(): call(pack_kernel, [shape((2 * count, HEAD_WIDTH), jnp.bfloat16)], [HBM] *...  0.78 us
  transfers between devices with their start and end apart: 6, of which 4 were waited for; matrix products, arithmetic and copies ran while one was open for 0% of the time, Pallas kernels for 17%

profile of v3, /device:TPU:0, one launch (start us, length us, event | category | flops | bytes accessed | tf_op | source)
XLA Modules:
  0.0 19.5 jit_solution(13082225546722274132)
XLA Ops:
  0.6 0.8 %shard_map.104 = bf16[192,128]{1,0:T(8,128)(2,1)S(1)} custom-call(bf16[96,128]{1,0:T(8,128)(2,1)} %tk_ref.1, bf16[96,128]{1,0:T(8,128)(2,1)} %tv_ref.1), custom_call_target="tpu_custom_call" | custom-call | bytes 98304 | tf_op jit(solution)/shard_map/pallas_call | solution.py:279
  1.4 3.1 %collective-permute-start = (bf16[192,128]{1,0:T(8,128)(2,1)S(1)}, bf16[192,128]{1,0:T(8,128)(2,1)S(1)}, u32[]{:S(2)}, u32[]{:S(2)}) collective-permute-start(bf16[192,128]{1,0:T(8,128)(2,1)S(1)} %shard_map.104), channel_id=1, source_target_pairs={{0,16},{16,0},{1,17},{17,1},{2,18},{18,2},{3,19},{19,3},{4,20},{20... | collective-permute-start | bytes 147464 | tf_op jit(solution)/shard_map/ppermute | solution.py:287
  4.5 2.0 %shard_map.103 = (bf16[1,128,1024]{2,1,0:T(8,128)(2,1)S(1)}, bf16[1,128,1024]{2,1,0:T(8,128)(2,1)S(1)}, bf16[224,128]{1,0:T(8,128)(2,1)S(1)}, f32[224,1024]{1,0:...) custom-call(s32[1]{0:T(128)} %bitcast.part_ref, s32[1,1,3]{2,1,0:T(1,128)} %mask_in.1, ...), custom_call_target="tpu_custom_call" | custom-call | flops 117440512 | bytes 786432 | tf_op jit(solution)/shard_map/pallas_call | solution.py:288
  6.5 0.1 collective-permute-done.kv_ref
  6.5 0.6 %shard_map.105 = (bf16[96,256]{1,0:T(8,128)(2,1)S(1)}, bf16[96,1024]{1,0:T(8,128)(2,1)S(1)}, f32[8,1024]{1,0:T(8,128)S(1)}) custom-call(bf16[1,128,1024]{2,1,0:T(8,128)(2,1)S(1)} %get-tuple-element.16.q_ref, bf16[1,128,1024]{2,1,0:T(8,128)(2,1)S(1)} %get-tuple-element.17.g_ref, bf16[192,128]{1,0:T(8,128)(2,1)S(1)} %collective-permute-done.kv_ref, ...), custom_call_target="tpu_custom_call" | custom-call | flops 100663296 | bytes 524288 | tf_op jit(solution)/shard_map/pallas_call | solution.py:321
  7.2 2.1 %collective-permute-start.1 = (bf16[96,256]{1,0:T(8,128)(2,1)S(1)}, bf16[96,256]{1,0:T(8,128)(2,1)S(1)}, u32[]{:S(2)}, u32[]{:S(2)}) collective-permute-start(bf16[96,256]{1,0:T(8,128)(2,1)S(1)} %get-tuple-element.28), channel_id=1, source_target_pairs={{0,16},{16,0},{1,17},{17,1},{2,18},{18,2},{3,19},{19,3},{4,20},{20... | collective-permute-start | bytes 147464 | tf_op jit(solution)/shard_map/ppermute | solution.py:332
  9.3 1.3 %shard_map.106 = (bf16[1,128,1024]{2,1,0:T(8,128)(2,1)}, bf16[1,128,256]{2,1,0:T(8,128)(2,1)}, bf16[96,256]{1,0:T(8,128)(2,1)S(1)}) custom-call(bf16[1,128,1024]{2,1,0:T(8,128)(2,1)S(1)} %get-tuple-element.16.q_ref, bf16[1,128,1024]{2,1,0:T(8,128)(2,1)S(1)} %get-tuple-element.17.g_ref, bf16[224,128]{1,0:T(8,128)(2,1)S(1)} %get-tuple-element.18.near_ref, ...), custom_call_target="tpu_custom_call" | custom-call | flops 201326592 | bytes 786432 | tf_op jit(solution)/shard_map/pallas_call | solution.py:333
  10.6 0.8 %collective-permute-done.1 = bf16[96,256]{1,0:T(8,128)(2,1)S(1)} collective-permute-done((bf16[96,256]{1,0:T(8,128)(2,1)S(1)}, bf16[96,256]{1,0:T(8,128)(2,1)S(1)}, u32[]{:S(2)}, u32[]{:S(2)}) %collective-permute-start.1) | collective-permute-done | bytes 49184 | tf_op jit(solution)/shard_map/ppermute | solution.py:332
  11.4 0.6 %collective-permute-start.3 = (bf16[48,256]{1,0:T(8,128)(2,1)S(1)}, bf16[48,256]{1,0:T(8,128)(2,1)S(1)}, u32[]{:S(2)}, u32[]{:S(2)}) collective-permute-start(bf16[48,256]{1,0:T(8,128)(2,1)S(1)} %get-tuple-element.30), channel_id=1, source_target_pairs={{0,9},{1,8},{2,11},{3,10},{4,13},{5,12},{6,15},{7,14},{8,1},{9,0},... | collective-permute-start | bytes 73736 | tf_op jit(solution)/shard_map/ppermute | solution.py:243
  12.0 2.6 %collective-permute-start.2 = (bf16[48,256]{1,0:T(8,128)(2,1)S(1)}, bf16[48,256]{1,0:T(8,128)(2,1)S(1)}, u32[]{:S(2)}, u32[]{:S(2)}) collective-permute-start(bf16[48,256]{1,0:T(8,128)(2,1)S(1)} %get-tuple-element.29), channel_id=1, source_target_pairs={{0,1},{1,0},{2,3},{3,2},{4,5},{5,4},{6,7},{7,6},{8,9},{9,8},{10,11... | collective-permute-start | bytes 73736 | tf_op jit(solution)/shard_map/ppermute | solution.py:254
  14.7 0.9 %collective-permute-done.3 = bf16[48,256]{1,0:T(8,128)(2,1)S(1)} collective-permute-done((bf16[48,256]{1,0:T(8,128)(2,1)S(1)}, bf16[48,256]{1,0:T(8,128)(2,1)S(1)}, u32[]{:S(2)}, u32[]{:S(2)}) %collective-permute-start.3) | collective-permute-done | bytes 24608 | tf_op jit(solution)/shard_map/ppermute | solution.py:243
  15.6 0.0 collective-permute-done.2
  15.6 1.9 %collective-permute-start.5 = (bf16[24,256]{1,0:T(8,128)(2,1)S(1)}, bf16[24,256]{1,0:T(8,128)(2,1)S(1)}, u32[]{:S(2)}, u32[]{:S(2)}) collective-permute-start(bf16[24,256]{1,0:T(8,128)(2,1)S(1)} %get-tuple-element.32), channel_id=1, source_target_pairs={{0,5},{1,4},{2,7},{3,6},{4,1},{5,0},{6,3},{7,2},{8,13},{9,12},{10,... | collective-permute-start | bytes 36872 | tf_op jit(solution)/shard_map/ppermute | solution.py:243
  17.5 0.4 %collective-permute-start.4 = (bf16[24,256]{1,0:T(8,128)(2,1)S(1)}, bf16[24,256]{1,0:T(8,128)(2,1)S(1)}, u32[]{:S(2)}, u32[]{:S(2)}) collective-permute-start(bf16[24,256]{1,0:T(8,128)(2,1)S(1)} %get-tuple-element.31), channel_id=1, source_target_pairs={{0,1},{1,0},{2,3},{3,2},{4,5},{5,4},{6,7},{7,6},{8,9},{9,8},{10,11... | collective-permute-start | bytes 36872 | tf_op jit(solution)/shard_map/ppermute | solution.py:254
  17.9 1.0 %collective-permute-done.5 = bf16[24,256]{1,0:T(8,128)(2,1)S(1)} collective-permute-done((bf16[24,256]{1,0:T(8,128)(2,1)S(1)}, bf16[24,256]{1,0:T(8,128)(2,1)S(1)}, u32[]{:S(2)}, u32[]{:S(2)}) %collective-permute-start.5) | collective-permute-done | bytes 12320 | tf_op jit(solution)/shard_map/ppermute | solution.py:243
  18.9 0.0 collective-permute-done.4
  18.9 0.6 %add_convert_fusion.2 = bf16[24,256]{1,0:T(8,128)(2,1)} fusion(bf16[24,256]{1,0:T(8,128)(2,1)S(1)} %collective-permute-done.5, bf16[24,256]{1,0:T(8,128)(2,1)S(1)} %collective-permute-done.4), kind=kLoop, calls=%fused_computation.2 | loop fusion | flops 24576 | bytes 36864 | tf_op jit(solution)/shard_map/convert_element_type | solution.py:255
  (4 shorter events, 0.0 us)
Async XLA Ops:
  1.4 5.1 %collective-permute-start = (bf16[192,128]{1,0:T(8,128)(2,1)S(1)}, bf16[192,128]{1,0:T(8,128)(2,1)S(1)}, u32[]{:S(2)}, u32[]{:S(2)}) collective-permute-start(bf16[192,128]{1,0:T(8,128)(2,1)S(1)} %shard_map.104), channel_id=1, source_target_pairs={{0,16},{16,0},{1,17},{17,1},{2,18},{18,2},{3,19},{19,3},{4,20},{20... | collective-permute-start | bytes 147464 | tf_op jit(solution)/shard_map/ppermute | solution.py:287
  7.2 4.2 %collective-permute-start.1 = (bf16[96,256]{1,0:T(8,128)(2,1)S(1)}, bf16[96,256]{1,0:T(8,128)(2,1)S(1)}, u32[]{:S(2)}, u32[]{:S(2)}) collective-permute-start(bf16[96,256]{1,0:T(8,128)(2,1)S(1)} %get-tuple-element.28), channel_id=1, source_target_pairs={{0,16},{16,0},{1,17},{17,1},{2,18},{18,2},{3,19},{19,3},{4,20},{20... | collective-permute-start | bytes 147464 | tf_op jit(solution)/shard_map/ppermute | solution.py:332
  11.4 4.2 %collective-permute-start.3 = (bf16[48,256]{1,0:T(8,128)(2,1)S(1)}, bf16[48,256]{1,0:T(8,128)(2,1)S(1)}, u32[]{:S(2)}, u32[]{:S(2)}) collective-permute-start(bf16[48,256]{1,0:T(8,128)(2,1)S(1)} %get-tuple-element.30), channel_id=1, source_target_pairs={{0,9},{1,8},{2,11},{3,10},{4,13},{5,12},{6,15},{7,14},{8,1},{9,0},... | collective-permute-start | bytes 73736 | tf_op jit(solution)/shard_map/ppermute | solution.py:243
  12.0 3.6 %collective-permute-start.2 = (bf16[48,256]{1,0:T(8,128)(2,1)S(1)}, bf16[48,256]{1,0:T(8,128)(2,1)S(1)}, u32[]{:S(2)}, u32[]{:S(2)}) collective-permute-start(bf16[48,256]{1,0:T(8,128)(2,1)S(1)} %get-tuple-element.29), channel_id=1, source_target_pairs={{0,1},{1,0},{2,3},{3,2},{4,5},{5,4},{6,7},{7,6},{8,9},{9,8},{10,11... | collective-permute-start | bytes 73736 | tf_op jit(solution)/shard_map/ppermute | solution.py:254
  15.6 3.3 %collective-permute-start.5 = (bf16[24,256]{1,0:T(8,128)(2,1)S(1)}, bf16[24,256]{1,0:T(8,128)(2,1)S(1)}, u32[]{:S(2)}, u32[]{:S(2)}) collective-permute-start(bf16[24,256]{1,0:T(8,128)(2,1)S(1)} %get-tuple-element.32), channel_id=1, source_target_pairs={{0,5},{1,4},{2,7},{3,6},{4,1},{5,0},{6,3},{7,2},{8,13},{9,12},{10,... | collective-permute-start | bytes 36872 | tf_op jit(solution)/shard_map/ppermute | solution.py:243
  17.5 1.4 %collective-permute-start.4 = (bf16[24,256]{1,0:T(8,128)(2,1)S(1)}, bf16[24,256]{1,0:T(8,128)(2,1)S(1)}, u32[]{:S(2)}, u32[]{:S(2)}) collective-permute-start(bf16[24,256]{1,0:T(8,128)(2,1)S(1)} %get-tuple-element.31), channel_id=1, source_target_pairs={{0,1},{1,0},{2,3},{3,2},{4,5},{5,4},{6,7},{7,6},{8,9},{9,8},{10,11... | collective-permute-start | bytes 36872 | tf_op jit(solution)/shard_map/ppermute | solution.py:254
